TPU v7x, 256 devices: a whole 4x4x8 slice. The times are simulated.
256 devices in a mesh: sens: 4 (over x_lo, core), src: 64 (over z, x_hi, y).
Axes of the slice: x: 4 (x_hi: 2, x_lo: 2; x = x_hi * 2 + x_lo), y: 4, z: 8, core: 2. Of those that a mesh axis runs over, the one named last changes fastest.
Arguments:
- operator: bfloat16 [128, 2, 512, 8192], P(None, None, 'sens', 'src'), may hold values from -0.75 to 0.75
- right_side: float32 [128, 2, 32, 8192], P('sens', None, None, 'src'), may hold values from -6 to 6
- noise_weights: float32 [128, 512], P('src', 'sens'), may hold values from 0.25 to 4
- damping: float32 [128], P('sens'), may hold values from 1 to 16
Outputs:
- solution: float32 [128, 2, 32, 8192], P('sens', None, None, 'src')
- residual: float32 [128, 2, 32, 8192], P('sens', None, None, 'src')
All inputs are finite; a program needn't handle non-finite values.
Results may differ from a plain program's by a relative error of at most 0.025.
Values may be sent and summed in bfloat16 or wider, within the bound.
A program may use at most 128 MiB of HBM per device.

v0:
```python
import functools

import jax
import jax.numpy as jnp
from jax import lax
from jax.sharding import Mesh
from jax.sharding import PartitionSpec as P

ITERS = 2
SENS = ("sens_0", "sens_1")
SRC = ("src_0", "src_1", "src_2")
SENS_SRC = ("sens_0", "sens_1", "src_0", "src_1", "src_2")


def copy_for_each(value, axis):
    copies = jnp.broadcast_to(value, (lax.axis_size(axis), *value.shape))
    return lax.all_to_all(copies, axis, split_axis=0, concat_axis=0, tiled=True)


def laid_out(pieces, dim):
    pieces = jnp.moveaxis(pieces, 0, dim)
    shape = pieces.shape
    return pieces.reshape(*shape[:dim], shape[dim] * shape[dim + 1], *shape[dim + 2 :])


def gathered_copies(value, axis, dim):
    pieces = copy_for_each(value, axis)
    return laid_out(pieces, dim)


def in_blocks(value, dim, size):
    before, after = (value.shape[:dim], value.shape[dim + 1 :])
    return jnp.moveaxis(value.reshape(*before, size, -1, *after), dim, 0)


def sent_and_summed(value, axis, dim):
    size = lax.axis_size(axis)
    pieces = lax.all_to_all(in_blocks(value, dim, size), axis, 0, 0, tiled=True)
    return jnp.sum(pieces.astype(jnp.float32), axis=0)


def cut_rows(length, count):
    unit = 8 if length >= 8 * count else 1
    return [length // unit * k // count * unit for k in range(1, count)]


def exchange_in_pieces(value, axis, pieces, split_dim, concat_dim):
    blocks = in_blocks(value, split_dim, lax.axis_size(axis))
    widest = max(range(1, max(2, blocks.ndim - 1)), key=lambda d: blocks.shape[d])
    finished = []
    for share in jnp.split(blocks, cut_rows(blocks.shape[widest], pieces), axis=widest):
        if share.size:
            finished.append(lax.all_to_all(share, axis, split_axis=0, concat_axis=0, tiled=True))
    return laid_out(jnp.concatenate(finished, axis=widest), concat_dim)


def by_axis(value, axes):
    return functools.reduce(lax.psum, axes, value)


def in_one_piece(arrays, axis, split_dim, concat_dim, along):
    both = jnp.concatenate(arrays, axis=along)
    whole, at, finished = (
        lax.all_to_all(both, axis, split_axis=split_dim, concat_axis=concat_dim, tiled=True),
        0,
        [],
    )
    for a in arrays:
        finished.append(lax.slice_in_dim(whole, at, at + a.shape[along], axis=along))
        at += a.shape[along]
    return tuple(finished)


def forward_all(gmat, vector):
    real_part = jnp.einsum(
        "fms,frs->frm", gmat[:, 0], vector[:, 0], preferred_element_type=jnp.float32
    ) - jnp.einsum("fms,frs->frm", gmat[:, 1], vector[:, 1], preferred_element_type=jnp.float32)
    imag_part = jnp.einsum(
        "fms,frs->frm", gmat[:, 0], vector[:, 1], preferred_element_type=jnp.float32
    ) + jnp.einsum("fms,frs->frm", gmat[:, 1], vector[:, 0], preferred_element_type=jnp.float32)
    return jnp.stack([real_part, imag_part], axis=1)


def adjoint_all(gmat, field):
    real_part = jnp.einsum(
        "fms,frm->frs", gmat[:, 0], field[:, 0], preferred_element_type=jnp.float32
    ) + jnp.einsum("fms,frm->frs", gmat[:, 1], field[:, 1], preferred_element_type=jnp.float32)
    imag_part = jnp.einsum(
        "fms,frm->frs", gmat[:, 0], field[:, 1], preferred_element_type=jnp.float32
    ) - jnp.einsum("fms,frm->frs", gmat[:, 1], field[:, 0], preferred_element_type=jnp.float32)
    return jnp.stack([real_part, imag_part], axis=1)


def freq_hessian(moved, noise_weights, local_damping, vector):
    rounded = vector.astype(jnp.bfloat16)
    spectra = gathered_copies(rounded, SENS, 2)
    sensor_field = forward_all(moved, spectra)
    weighted = (noise_weights[:, None, None, :] * sensor_field).astype(jnp.bfloat16)
    back = sent_and_summed(adjoint_all(moved, weighted).astype(jnp.bfloat16), SENS, 2)
    return back + local_damping[:, None, None, None] * vector


def body(operator, right_side, noise_weights, damping):
    moved = exchange_in_pieces(operator, SRC, 2, 0, 3)
    start = lax.all_to_all(
        lax.all_to_all(
            right_side.astype(jnp.bfloat16), SENS, split_axis=2, concat_axis=0, tiled=True
        ),
        SRC,
        split_axis=0,
        concat_axis=3,
        tiled=True,
    ).astype(right_side.dtype)
    damping_full = gathered_copies(damping, SENS, 0)
    count = moved.shape[0]
    local_damping = lax.dynamic_slice_in_dim(damping_full, lax.axis_index(SRC) * count, count, 0)
    solution = jnp.zeros_like(start)
    residual = start
    direction = start
    norm_now = by_axis(jnp.sum(residual * residual), SENS_SRC)
    for step in range(ITERS):
        image = freq_hessian(moved, noise_weights, local_damping, direction)
        curve, cross, square = (
            by_axis(jnp.sum(direction * image), SENS_SRC),
            by_axis(jnp.sum(residual * image), SENS_SRC),
            by_axis(jnp.sum(image * image), SENS_SRC),
        )
        alpha = norm_now / curve
        solution = solution + alpha * direction
        residual = residual - alpha * image
        norm_next = norm_now - 2.0 * alpha * cross + alpha * alpha * square
        if step + 1 < ITERS:
            direction = residual + norm_next / norm_now * direction
        norm_now = norm_next
    solution, residual = tuple(
        (
            part.astype(jnp.float32)
            for part in in_one_piece(
                (solution.astype(jnp.bfloat16), residual.astype(jnp.bfloat16)), SRC, 3, 0, 1
            )
        )
    )
    solution, residual = tuple(
        (
            part.astype(jnp.float32)
            for part in in_one_piece(
                (solution.astype(jnp.bfloat16), residual.astype(jnp.bfloat16)), SENS, 0, 2, 1
            )
        )
    )
    return (solution, residual)


def solution(mesh):
    split = Mesh(
        mesh.devices.reshape(2, 2, 8, 2, 4), ("sens_0", "sens_1", "src_0", "src_1", "src_2")
    )
    return jax.shard_map(
        body,
        mesh=split,
        in_specs=(P(None, None, SENS, SRC), P(SENS, None, None, SRC), P(SRC, SENS), P(SENS)),
        out_specs=(P(SENS, None, None, SRC), P(SENS, None, None, SRC)),
        check_vma=False,
    )
```

profile of v0, /device:TPU:2, one launch (start us, length us, event | category | flops | bytes accessed | tf_op | source)
XLA Modules:
  0.0 619.9 jit_solution(16046121974868913523)
XLA Ops:
  0.6 2.0 copy.103
  2.7 11.8 %all_to_all.108 = bf16[32,2,32,128]{3,1,0,2:T(2,128)(2,1)S(1)} all-to-all(bf16[32,2,32,128]{3,1,0,2:T(2,128)(2,1)S(1)} %copy.103), channel_id=1, replica_groups=mesh['sens_0'=2,'sens_1'=2,'src_0'=8,'src_1'=2,'src_2'=4] {'sens_0','sen..., dimensions={2} | all-to-all | bytes 1048576 | tf_op jit(solution)/shard_map/all_to_all | solution.py:106
  14.5 0.6 copy.105
  15.2 30.7 %all_to_all.109 = bf16[128,2,8,128]{3,2,1,0:T(8,128)(2,1)S(1)} all-to-all(bf16[128,2,8,128]{3,2,1,0:T(8,128)(2,1)S(1)} %bitcast.150), channel_id=1, replica_groups=mesh['sens_0'=2,'sens_1'=2,'src_0'=8,'src_1'=2,'src_2'=4] {'src_0','src_..., dimensions={0} | all-to-all | bytes 1048576 | tf_op jit(solution)/shard_map/all_to_all | solution.py:105
  46.4 1.6 broadcast_in_dim.6
  47.9 6.4 %all-to-all-start.4 = ((bf16[4,2,2,8,8192]{4,3,1,2,0:T(8,128)(2,1)}), bf16[4,2,2,8,8192]{4,3,1,2,0:T(8,128)(2,1)}, u32[]{:S(2)}, u32[]{:S(2)}) async-start(bf16[4,2,2,8,8192]{4,3,1,2,0:T(8,128)(2,1)} %broadcast_in_dim.6), calls=%async_computation.4 | async-start | bytes 4194304 | tf_op jit(solution)/shard_map/all_to_all | solution.py:17
  54.4 6.3 %fusion.34 = (bf16[64,2,2,64,128]{4,3,2,1,0:T(8,128)(2,1)S(1)}, bf16[64,2,2,64,128]{4,3,2,1,0:T(8,128)(2,1)}) fusion(bf16[64,2,2,128,128]{4,3,2,1,0:T(8,128)(2,1)} %bitcast.141), kind=kLoop, calls=%fused_computation.82 | loop fusion | bytes 16777216 | tf_op jit(solution)/shard_map/split | solution.py:51
  60.7 2.9 copy.46
  63.6 14.9 %all-to-all-done.4 = bf16[4,2,2,8,8192]{4,3,1,2,0:T(8,128)(2,1)} async-done(((bf16[4,2,2,8,8192]{4,3,1,2,0:T(8,128)(2,1)}), bf16[4,2,2,8,8192]{4,3,1,2,0:T(8,128)(2,1)}, u32[]{:S(2)}, u32[]{:S(2)}) %all-to-all-start.4) | async-done | bytes 2097184 | tf_op jit(solution)/shard_map/all_to_all | solution.py:17
  78.5 6.5 %all-to-all-start.2 = ((bf16[64,2,2,64,128]{4,3,1,2,0:T(8,128)(2,1)}), bf16[64,2,2,64,128]{4,3,1,2,0:T(8,128)(2,1)}, u32[]{:S(2)}, u32[]{:S(2)}) async-start(bf16[64,2,2,64,128]{4,3,1,2,0:T(8,128)(2,1)} %copy.46), calls=%async_computation.2 | async-start | bytes 8388608 | tf_op jit(solution)/shard_map/all_to_all | solution.py:53
  85.0 5.5 copy.47
  90.5 89.8 %all-to-all-done.2 = bf16[64,2,2,64,128]{4,3,1,2,0:T(8,128)(2,1)} async-done(((bf16[64,2,2,64,128]{4,3,1,2,0:T(8,128)(2,1)}), bf16[64,2,2,64,128]{4,3,1,2,0:T(8,128)(2,1)}, u32[]{:S(2)}, u32[]{:S(2)}) %all-to-all-start.2) | async-done | bytes 4194336 | tf_op jit(solution)/shard_map/all_to_all | solution.py:53
  180.3 8.6 %all-to-all-start.3 = ((bf16[64,2,2,64,128]{4,3,1,2,0:T(8,128)(2,1)}), bf16[64,2,2,64,128]{4,3,1,2,0:T(8,128)(2,1)}, u32[]{:S(2)}, u32[]{:S(2)}) async-start(bf16[64,2,2,64,128]{4,3,1,2,0:T(8,128)(2,1)} %copy.47), calls=%async_computation.3 | async-start | bytes 8388608 | tf_op jit(solution)/shard_map/all_to_all | solution.py:53
  188.9 3.1 copy_bitcast_fusion.4
  192.0 91.3 %all-to-all-done.3 = bf16[64,2,2,64,128]{4,3,1,2,0:T(8,128)(2,1)} async-done(((bf16[64,2,2,64,128]{4,3,1,2,0:T(8,128)(2,1)}), bf16[64,2,2,64,128]{4,3,1,2,0:T(8,128)(2,1)}, u32[]{:S(2)}, u32[]{:S(2)}) %all-to-all-start.3) | async-done | bytes 4194336 | tf_op jit(solution)/shard_map/all_to_all | solution.py:53
  283.4 0.6 broadcast_in_dim.14
  283.9 3.3 all-to-all-start.6
  287.3 4.7 copy_bitcast_fusion
  292.0 1.5 fusion.23
  293.5 1.5 fusion.24
  295.0 1.5 fusion.11
  296.6 1.5 fusion.10
  298.1 0.7 fusion.30
  298.8 0.7 fusion.29
  299.5 0.8 fusion.7
  300.3 0.8 fusion.6
  301.0 1.5 copy_bitcast_fusion.2
  302.6 4.4 all-to-all-start.5
  307.0 0.5 broadcast.14
  307.6 0.6 reduce.7
  308.4 22.7 %all-to-all-done.5 = bf16[4,2,2,8,8192]{4,3,1,2,0:T(8,128)(2,1)} async-done(((bf16[4,2,2,8,8192]{4,3,1,2,0:T(8,128)(2,1)}), bf16[4,2,2,8,8192]{4,3,1,2,0:T(8,128)(2,1)}, u32[]{:S(2)}, u32[]{:S(2)}) %all-to-all-start.5) | async-done | bytes 2097184 | tf_op jit(solution)/shard_map/all_to_all | solution.py:38
  331.1 2.0 convert_reduce_fusion.1
  333.3 1.7 multiply_reduce_fusion
  335.0 5.6 all-reduce.4
  340.6 3.2 all-reduce.3
  343.7 16.8 %all-reduce = (f32[]{:T(128)}, f32[]{:T(128)}, f32[]{:T(128)}) all-reduce(f32[]{:T(128)} %get-tuple-element.14, f32[]{:T(128)} %get-tuple-element.15, f32[]{:T(128)} %get-tuple-element.16), channel_id=1, replica_groups=mesh['sens_0'=2,'sens_1'=2,'src_0'=8,'src_1'=2,'src_2'=4] {'src_0'}, use_global_device_ids=true, to_apply=%region_3.0 | all-reduce | flops 3 | bytes 24 | tf_op jit(solution)/shard_map/psum | solution.py:58
  360.6 7.1 %all-reduce.2 = (f32[]{:T(128)}, f32[]{:T(128)}, f32[]{:T(128)}) all-reduce(f32[]{:T(128)} %get-tuple-element.5, f32[]{:T(128)} %get-tuple-element.6, f32[]{:T(128)} %get-tuple-element.7), channel_id=1, replica_groups=mesh['sens_0'=2,'sens_1'=2,'src_0'=8,'src_1'=2,'src_2'=4] {'src_1'}, use_global_device_ids=true, to_apply=%region_4.0 | all-reduce | flops 3 | bytes 24 | tf_op jit(solution)/shard_map/psum | solution.py:58
  367.7 10.2 %all-reduce.1 = (f32[]{:T(128)}, f32[]{:T(128)}, f32[]{:T(128)}) all-reduce(f32[]{:T(128)} %get-tuple-element.11, f32[]{:T(128)} %get-tuple-element.12, f32[]{:T(128)} %get-tuple-element.13), channel_id=1, replica_groups=mesh['sens_0'=2,'sens_1'=2,'src_0'=8,'src_1'=2,'src_2'=4] {'src_2'}, use_global_device_ids=true, to_apply=%region_5.0 | all-reduce | flops 3 | bytes 24 | tf_op jit(solution)/shard_map/psum | solution.py:58
  381.5 0.3 fusion.31
  382.0 28.4 %all_to_all.110 = bf16[4,2,2,8,8192]{4,3,1,2,0:T(8,128)(2,1)S(1)} all-to-all(bf16[4,2,2,8,8192]{4,3,1,2,0:T(8,128)(2,1)S(1)} %broadcast_in_dim.15), channel_id=1, replica_groups=mesh['sens_0'=2,'sens_1'=2,'src_0'=8,'src_1'=2,'src_2'=4] {'sens_0','sen..., dimensions={0} | all-to-all | bytes 4194304 | tf_op jit(solution)/shard_map/all_to_all | solution.py:17
  410.6 3.9 fusion.25
  414.5 1.5 fusion.26
  416.0 1.5 fusion.9
  417.5 1.5 fusion.8
  419.1 0.7 fusion.28
  419.8 0.7 fusion.27
  420.4 0.7 fusion.5
  421.1 0.7 fusion.4
  422.0 28.3 %all_to_all.111 = bf16[4,2,2,8,8192]{4,3,1,2,0:T(8,128)(2,1)S(1)} all-to-all(bf16[4,2,2,8,8192]{4,3,1,2,0:T(8,128)(2,1)S(1)} %copy_bitcast_fusion.1), channel_id=1, replica_groups=mesh['sens_0'=2,'sens_1'=2,'src_0'=8,'src_1'=2,'src_2'=4] {'sens_0','sen..., dimensions={0} | all-to-all | bytes 4194304 | tf_op jit(solution)/shard_map/all_to_all | solution.py:38
  450.3 0.3 convert_reduce_fusion
  450.8 1.7 fusion.22
  452.5 5.5 psum.170
  458.1 3.1 psum.171
  461.1 16.2 %psum.172 = f32[]{:T(128)} all-reduce(f32[]{:T(128)} %psum.171), channel_id=1, replica_groups=mesh['sens_0'=2,'sens_1'=2,'src_0'=8,'src_1'=2,'src_2'=4] {'src_0'}, use_global_device_ids=true, to_apply=%region_23.0 | all-reduce | flops 1 | bytes 8 | tf_op jit(solution)/shard_map/psum | solution.py:58
  477.3 7.0 %psum.173 = f32[]{:T(128)} all-reduce(f32[]{:T(128)} %psum.172), channel_id=1, replica_groups=mesh['sens_0'=2,'sens_1'=2,'src_0'=8,'src_1'=2,'src_2'=4] {'src_1'}, use_global_device_ids=true, to_apply=%region_24.0 | all-reduce | flops 1 | bytes 8 | tf_op jit(solution)/shard_map/psum | solution.py:58
  484.4 8.9 %psum.174 = f32[]{:T(128)} all-reduce(f32[]{:T(128)} %psum.173), channel_id=1, replica_groups=mesh['sens_0'=2,'sens_1'=2,'src_0'=8,'src_1'=2,'src_2'=4] {'src_2'}, use_global_device_ids=true, to_apply=%region_25.0 | all-reduce | flops 1 | bytes 8 | tf_op jit(solution)/shard_map/psum | solution.py:58
  494.0 1.6 fusion.13
  495.7 16.0 %copy.64 = bf16[2,4,8,8192]{2,1,0,3:T(4,128)(2,1)} copy(bf16[2,4,8,8192]{3,2,0,1:T(8,128)(2,1)S(1)} %pad_maximum_fusion.2) | data formatting | bytes 2097152 | tf_op jit(solution)/shard_map/concatenate | solution.py:62
  511.7 19.8 %reshape.61 = bf16[64,2,4096]{2,1,0:T(2,128)(2,1)S(1)} reshape(bf16[8192,2,4,8]{3,2,1,0:T(4,128)(2,1)} %bitcast.135) | data formatting | bytes 2097152
  531.6 30.0 %all_to_all.112 = bf16[64,2,4096]{2,1,0:T(2,128)(2,1)S(1)} all-to-all(bf16[64,2,4096]{2,1,0:T(2,128)(2,1)S(1)} %reshape.61), channel_id=1, replica_groups=mesh['sens_0'=2,'sens_1'=2,'src_0'=8,'src_1'=2,'src_2'=4] {'src_0','src_..., dimensions={0} | all-to-all | bytes 2097152 | tf_op jit(solution)/shard_map/all_to_all | solution.py:64
  561.6 20.8 %reshape.62 = bf16[8192,2,4,8]{3,2,1,0:T(4,128)(2,1)} reshape(bf16[64,2,4096]{2,1,0:T(2,128)(2,1)S(1)} %all_to_all.112) | data formatting | bytes 2097152
  582.4 18.1 %copy.75 = bf16[2,4,8,64,128]{4,2,1,0,3:T(8,128)(2,1)S(1)} copy(bf16[2,4,8,64,128]{2,1,0,4,3:T(4,128)(2,1)} %bitcast.136) | data formatting | bytes 2097152 | tf_op jit(solution)/shard_map/all_to_all | solution.py:64
  600.5 17.5 %all_to_all.113 = bf16[128,4,8,128]{3,2,1,0:T(8,128)(2,1)S(1)} all-to-all(bf16[128,4,8,128]{3,2,1,0:T(8,128)(2,1)S(1)} %bitcast.146), channel_id=1, replica_groups=mesh['sens_0'=2,'sens_1'=2,'src_0'=8,'src_1'=2,'src_2'=4] {'sens_0','sen..., dimensions={0} | all-to-all | bytes 2097152 | tf_op jit(solution)/shard_map/all_to_all | solution.py:64
  618.2 1.6 slice_convert_fusion
  (34 shorter events, 2.0 us)
Async XLA Ops:
  45.9 287.4 %copy-start.2 = (bf16[128,2,8,128]{3,2,1,0:T(8,128)(2,1)}, bf16[128,2,8,128]{3,2,1,0:T(8,128)(2,1)S(1)}, u32[]{:S(2)}) copy-start(bf16[128,2,8,128]{3,2,1,0:T(8,128)(2,1)S(1)} %all_to_all.109) | copy-start | bytes 1572868
  46.3 335.2 %copy-start.1 = (bf16[2,2,8,8192]{3,2,0,1:T(8,128)(2,1)}, bf16[2,2,8,8192]{3,2,0,1:T(8,128)(2,1)S(1)}, u32[]{:S(2)}) copy-start(bf16[2,2,8,8192]{3,2,0,1:T(8,128)(2,1)S(1)} %reshape.51) | copy-start | bytes 1572868
  47.9 30.6 %all-to-all-start.4 = ((bf16[4,2,2,8,8192]{4,3,1,2,0:T(8,128)(2,1)}), bf16[4,2,2,8,8192]{4,3,1,2,0:T(8,128)(2,1)}, u32[]{:S(2)}, u32[]{:S(2)}) async-start(bf16[4,2,2,8,8192]{4,3,1,2,0:T(8,128)(2,1)} %broadcast_in_dim.6), calls=%async_computation.4 | async-start | bytes 4194304 | tf_op jit(solution)/shard_map/all_to_all | solution.py:17
  78.5 101.8 %all-to-all-start.2 = ((bf16[64,2,2,64,128]{4,3,1,2,0:T(8,128)(2,1)}), bf16[64,2,2,64,128]{4,3,1,2,0:T(8,128)(2,1)}, u32[]{:S(2)}, u32[]{:S(2)}) async-start(bf16[64,2,2,64,128]{4,3,1,2,0:T(8,128)(2,1)} %copy.46), calls=%async_computation.2 | async-start | bytes 8388608 | tf_op jit(solution)/shard_map/all_to_all | solution.py:53
  180.3 103.1 %all-to-all-start.3 = ((bf16[64,2,2,64,128]{4,3,1,2,0:T(8,128)(2,1)}), bf16[64,2,2,64,128]{4,3,1,2,0:T(8,128)(2,1)}, u32[]{:S(2)}, u32[]{:S(2)}) async-start(bf16[64,2,2,64,128]{4,3,1,2,0:T(8,128)(2,1)} %copy.47), calls=%async_computation.3 | async-start | bytes 8388608 | tf_op jit(solution)/shard_map/all_to_all | solution.py:53
  188.9 94.5 %copy-start.6 = (f32[32]{0:T(128)S(1)}, f32[32]{0:T(128)}, u32[]{:S(2)}) copy-start(f32[32]{0:T(128)} %param.7) | copy-start | bytes 388
  283.9 18.6 %all-to-all-start.6 = ((f32[4,1,32]{2,1,0:T(1,128)}), f32[4,1,32]{2,1,0:T(1,128)S(1)}, u32[]{:S(2)}, u32[]{:S(2)}) async-start(f32[4,1,32]{2,1,0:T(1,128)} %broadcast_in_dim.14), calls=%async_computation.6 | async-start | bytes 4096 | tf_op jit(solution)/shard_map/all_to_all | solution.py:17
  287.3 4.7 copy-start.4
  292.0 8.3 %copy-start = (bf16[2,2,128,8192]{3,2,0,1:T(8,128)(2,1)}, bf16[2,2,128,8192]{3,2,0,1:T(8,128)(2,1)S(1)}, u32[]{:S(2)}) copy-start(bf16[2,2,128,8192]{3,2,0,1:T(8,128)(2,1)S(1)} %copy_bitcast_fusion) | copy-start | bytes 25165828
  296.5 1.6 copy-start.5
  302.6 28.5 %all-to-all-start.5 = ((bf16[4,2,2,8,8192]{4,3,1,2,0:T(8,128)(2,1)}), bf16[4,2,2,8,8192]{4,3,1,2,0:T(8,128)(2,1)}, u32[]{:S(2)}, u32[]{:S(2)}) async-start(bf16[4,2,2,8,8192]{4,3,1,2,0:T(8,128)(2,1)} %copy_bitcast_fusion.2), calls=%async_computation.5 | async-start | bytes 4194304 | tf_op jit(solution)/shard_map/all_to_all | solution.py:38
  381.8 32.6 %slice-start = ((s8[8388608]{0:T(1024)(128)(4,1)}), s8[4194304]{0:T(1024)(128)(4,1)S(1)}, s32[]{:S(2)}) async-start(s8[8388608]{0:T(1024)(128)(4,1)} %bitcast.133), calls=%async_computation.11 | async-start | bytes 8388608
  410.4 4.0 slice-start.1
  422.0 28.8 %copy-start.3 = (bf16[128,2,8,128]{3,2,1,0:T(8,128)(2,1)S(1)}, bf16[128,2,8,128]{3,2,1,0:T(8,128)(2,1)}, u32[]{:S(2)}) copy-start(bf16[128,2,8,128]{3,2,1,0:T(8,128)(2,1)} %copy-done.2) | copy-start | bytes 1572868
where the time goes:
time: 623 us; the launch traced here: 620 us
  blocking collectives  230 us (37%)
  waiting for transfers between devices  219 us (35%)
  local copies, waits for them, and re-layouts  99.8 us (16%)
  starting transfers between devices  29.3 us (5%)
  matrix products  20.2 us (3%)
  other arithmetic  16.4 us (3%)
    all_to_all x2, waiting for transfers between devices, exchange_in_pieces(): lax.all_to_all(share, axis, split_axis=0, concat_axis=0, tiled=True)  181 us
    psum x10, blocking collectives, by_axis(): return functools.reduce(lax.psum, axes, value)  83.6 us
    all_to_all x2, blocking collectives, in_one_piece(): lax.all_to_all(both, axis, split_axis=split_dim, concat_axis=concat_dim,...  47.5 us
    unnamed x23, local copies, waits for them, and re-layouts  43.1 us
    all_to_all x1, blocking collectives, body(): lax.all_to_all(lax.all_to_all(right_side.astype(jnp.bfloat16), SENS, spli...  30.7 us
    all_to_all x1, blocking collectives, copy_for_each(): return lax.all_to_all(copies, axis, split_axis=0, concat_axis=0, tiled=True)  28.4 us
    all_to_all x1, blocking collectives, sent_and_summed(): pieces = lax.all_to_all(in_blocks(value, dim, size), axis, 0, 0, tiled=True)  28.3 us
    all_to_all x1, waiting for transfers between devices, sent_and_summed(): pieces = lax.all_to_all(in_blocks(value, dim, size), axis, 0, 0, tiled=True)  22.7 us
  transfers between devices with their start and end apart: 5, of which 4 were waited for; matrix products, arithmetic and copies ran while one was open for 6% of the time, Pallas kernels for 0%

commit v1 on v0

v1 whole, which is shorter than its diff:
```python
import functools

import jax
import jax.numpy as jnp
from jax import lax
from jax.experimental import pallas as pl
from jax.experimental.pallas import tpu as pltpu
from jax.sharding import PartitionSpec as P

BF16, F32 = jnp.bfloat16, jnp.float32
MESH = pl.DeviceIdType.MESH
NZ, NX, NY, NS = 8, 2, 4, 4
WAVES, ROWS, LANES = 2, 64, 128
OWN = 16
AXES = (("y", "z"), ("z", "y"))
SIZE = {"y": NY, "z": NZ}
STEPS = 8


def flip(value, bit):
    return value + bit - 2 * bit * lax.rem(lax.div(value, bit), 2)


def kernel(
    op_hbm, b_ref, w_ref, d_ref, sol_ref, res_ref,
    op, spectra, part, part2, field0, field1, out, grad, core_in, x_in, xh_out, xh_in,
    image0, image1, w_all, ring_y0, ring_z0, ring_z1, ring_y1, sums, sums_in,
    op_sem, sens_s, sens_r, rs_s, rs_r, ag_s, ag_r, xh_s, xh_r, w_s, w_r, sum_s, sum_r,
):
    s, q = lax.axis_index("sens"), lax.axis_index("src")
    z, xh, y = lax.div(q, 8), lax.rem(lax.div(q, 4), 2), lax.rem(q, 4)
    at = {"y": y, "z": z}
    rings = ((ring_y0, ring_z0), (ring_z1, ring_y1))

    def device(s=s, z=z, xh=xh, y=y):
        return (s, z * 8 + xh * 4 + y)

    def along(axis, step):
        n = SIZE[axis]
        return device(**{axis: lax.rem(at[axis] + n + step, n)})

    core_peer, x_peer, xh_peer = device(s=flip(s, 1)), device(s=flip(s, 2)), device(xh=1 - xh)
    sum_peers = (
        core_peer, x_peer, xh_peer, device(y=flip(y, 1)), device(y=flip(y, 2)),
        device(z=flip(z, 1)), device(z=flip(z, 2)), device(z=flip(z, 4)),
    )
    greeted = (
        core_peer, x_peer, xh_peer, along("y", 1), along("y", -1), device(y=flip(y, 2)),
        along("z", 1), along("z", -1), device(z=flip(z, 2)), device(z=flip(z, 4)),
    )

    def copy_of(src, dst, send_sem, recv_sem, to):
        return pltpu.make_async_remote_copy(
            src_ref=src, dst_ref=dst, send_sem=send_sem, recv_sem=recv_sem,
            device_id=to, device_id_type=MESH,
        )

    def send(*args):
        copy = copy_of(*args)
        copy.start()
        return copy

    load = pltpu.make_async_copy(op_hbm, op, op_sem)
    load.start()
    barrier = pltpu.get_barrier_semaphore()
    for peer in greeted:
        pl.semaphore_signal(barrier, inc=1, device_id=peer, device_id_type=MESH)

    def round_own(wave):
        def step(i, _):
            spectra[wave, s, i] = b_ref[2 * i + wave].astype(BF16)
            return 0
        lax.fori_loop(0, OWN, step, 0)

    for wave in range(WAVES):
        round_own(wave)
    w_all[xh] = jnp.broadcast_to(w_ref[...][:, None, :], (2, 8, LANES))
    pl.semaphore_wait(barrier, len(greeted))
    w_copy = send(w_all.at[xh], w_all.at[xh], w_s, w_r, xh_peer)

    def place(wave, zz, xx, yy):
        return yy * 16 + zz * 2 + xx if wave == 0 else zz * 8 + yy * 2 + xx

    def indices(block, i):
        return 2 * block + lax.div(i, 8), lax.rem(lax.div(i, 4), 2), lax.rem(i, 4)

    def forward(wave, block):
        def step(i, _):
            zz, xx, yy = indices(block, i)
            out_ = lax.dot_general(
                spectra[wave, block, i], op[16 * zz + 8 * xx + 2 * yy + wave],
                (((1,), (1,)), ((), ())), preferred_element_type=F32,
            )
            real = out_[:32, :LANES] - out_[32:, LANES:]
            imag = out_[32:, :LANES] + out_[:32, LANES:]
            part[wave, place(wave, zz, xx, yy)] = jnp.concatenate([real, imag], axis=0).astype(BF16)
            return 0
        lax.fori_loop(0, OWN, step, 0, unroll=4)

    def adjoint(wave, block):
        def step(i, _):
            zz, xx, yy = indices(block, i)
            u = out[wave, place(wave, zz, xx, yy)]
            turned = jnp.concatenate([u[32:], -u[:32]], axis=0)
            f = 16 * zz + 8 * xx + 2 * yy + wave
            g = jnp.dot(u, op[f, :LANES], preferred_element_type=F32)
            g += jnp.dot(turned, op[f, LANES:], preferred_element_type=F32)
            grad[wave, block, i] = g.astype(BF16)
            return 0
        lax.fori_loop(0, OWN, step, 0, unroll=4)

    def sens_forward(wave):
        mine, core, far, both = s, flip(s, 1), flip(s, 2), flip(flip(s, 1), 2)

        def move(k, block, to):
            ref = spectra.at[wave, block]
            return copy_of(ref, ref, sens_s.at[wave, k], sens_r.at[wave, k], to)

        sent = [move(0, mine, x_peer), move(1, mine, core_peer), move(2, far, core_peer)]
        sent[0].start()
        sent[1].start()
        yield
        if wave == 0 and not started:
            load.wait()
            started.append(True)
        forward(wave, mine)
        move(1, core, core_peer).wait_recv()
        forward(wave, core)
        yield
        move(0, far, x_peer).wait_recv()
        sent[2].start()
        forward(wave, far)
        move(2, both, core_peer).wait_recv()
        forward(wave, both)
        for copy in sent:
            copy.wait_send()

    def ring_sum(wave, level, ref, result):
        axis = AXES[wave][level]
        n, me = SIZE[axis], at[axis]
        piece = ref.shape[0] // n
        half, ring = piece // 2, rings[wave][level]
        sent = []

        def span(base, h):
            return pl.ds(base * piece + h * half, half)

        def message(t, h, k):
            d = (1, -1)[k]
            dest = lax.rem(me + n + d * t, n)
            sems = (wave, level, k, t - 1, h)
            return copy_of(
                ref.at[span(dest, h)], ring.at[k, t - 1, pl.ds(h * half, half)],
                rs_s.at[sems], rs_r.at[sems], along(axis, d),
            )

        def go(t, h, k):
            copy = message(t, h, k)
            copy.start()
            sent.append(copy)

        def relay(t, h, k):
            message(t, h, k).wait_recv()
            dest = lax.rem(me + n + (1, -1)[k] * (t - 1), n)

            def add(i, _):
                at_ = dest * piece + h * half + i
                total = ref[at_].astype(F32) + ring[k, t - 1, h * half + i].astype(F32)
                ref[at_] = total.astype(BF16)
                return 0
            lax.fori_loop(0, half, add, 0, unroll=min(half, 2))
            go(t - 1, h, k)

        top = n // 2
        for k in (0, 1):
            go(top, k, k)
        for k in (0, 1):
            go(top - 1, 1 - k, k)
        yield
        for t in range(top, 1, -1):
            for k in (0, 1):
                relay(t, k, k)
            yield
            if t - 1 > 1:
                for k in (0, 1):
                    relay(t - 1, 1 - k, k)
                yield
        for h in (0, 1):
            for k in (0, 1):
                message(1, h, k).wait_recv()

        def last(i, _):
            total = ref[me * piece + i].astype(F32) + ring[0, 0, i].astype(F32)
            result(i, total + ring[1, 0, i].astype(F32))
            return 0
        lax.fori_loop(0, piece, last, 0, unroll=2)
        for copy in sent:
            copy.wait_send()

    def ring_gather(wave, level, ref):
        axis = AXES[wave][level]
        n, me = SIZE[axis], at[axis]
        piece = ref.shape[0] // n
        half = piece // 2
        sent = []

        def message(t, h, k, owner):
            sems = (wave, level, k, t - 1, h)
            where = ref.at[pl.ds(owner * piece + h * half, half)]
            return copy_of(where, where, ag_s.at[sems], ag_r.at[sems], along(axis, (1, -1)[k]))

        def go(t, h, k):
            copy = message(t, h, k, lax.rem(me + n - (1, -1)[k] * (t - 1), n))
            copy.start()
            sent.append(copy)

        def got(t, h, k):
            message(t, h, k, lax.rem(me + n - (1, -1)[k] * t, n)).wait_recv()

        top = n // 2
        for first in (0, 1):
            for k in (0, 1):
                go(1, k if first == 0 else 1 - k, k)
        yield
        for t in range(1, top):
            for k in (0, 1):
                got(t, k, k)
                go(t + 1, k, k)
            yield
            for k in (0, 1):
                got(t, 1 - k, k)
                if t + 1 < top:
                    go(t + 1, 1 - k, k)
            yield
        for k in (0, 1):
            got(top, k, k)
        for copy in sent:
            copy.wait_send()

    def reduce_field(wave, field):
        def keep2(i, total):
            part2[wave, i] = total.astype(BF16)

        def keep1(i, total):
            xh_out[wave, i] = total.astype(BF16)

        yield from ring_sum(wave, 0, part.at[wave], keep2)
        share = part2.at[wave, pl.ds(0, 64 // SIZE[AXES[wave][0]])]
        yield from ring_sum(wave, 1, share, keep1)
        copy = send(xh_out.at[wave], xh_in.at[wave], xh_s.at[wave], xh_r.at[wave], xh_peer)
        yield
        copy.wait_recv()
        field[wave] = xh_out[wave].astype(F32) + xh_in[wave].astype(F32)
        copy.wait_send()

    def spread(wave):
        outer, inner = AXES[wave]
        share = 64 // SIZE[outer]
        own = out.at[wave, pl.ds(at[outer] * share, share)]
        yield from ring_gather(wave, 1, own)
        yield from ring_gather(wave, 0, out.at[wave])

    def own_place(wave):
        return place(wave, z, 0, y)

    def sens_back(wave, image):
        mine, core, far, both = s, flip(s, 1), flip(s, 2), flip(flip(s, 1), 2)

        def to_core(k, block):
            return copy_of(
                grad.at[wave, block], core_in.at[wave, k],
                sens_s.at[wave, 3 + k], sens_r.at[wave, 3 + k], core_peer,
            )

        adjoint(wave, both)
        sent = [to_core(0, both)]
        sent[0].start()
        adjoint(wave, core)
        sent.append(to_core(1, core))
        sent[1].start()
        adjoint(wave, far)
        sent[0].wait_recv()

        def chip(i, _):
            total = grad[wave, far, i].astype(F32) + core_in[wave, 0, i].astype(F32)
            grad[wave, far, i] = total.astype(BF16)
            return 0
        lax.fori_loop(0, OWN, chip, 0, unroll=2)
        sent.append(send(
            grad.at[wave, far], x_in.at[wave], sens_s.at[wave, 5], sens_r.at[wave, 5], x_peer
        ))
        adjoint(wave, mine)
        yield
        sent[1].wait_recv()
        sent[2].wait_recv()

        def whole(i, _):
            total = grad[wave, mine, i].astype(F32) + core_in[wave, 1, i].astype(F32)
            image[2 * i + wave] = total + x_in[wave, i].astype(F32)
            return 0
        lax.fori_loop(0, OWN, whole, 0, unroll=2)
        for copy in sent:
            copy.wait_send()

    def folded(value):
        return jnp.sum(value.reshape(-1, 8, LANES), axis=0)

    def total_of(turn):
        sent = []
        for k in range(STEPS):
            copy = send(
                sums.at[turn, k], sums_in.at[turn, k], sum_s.at[turn, k], sum_r.at[turn, k],
                sum_peers[k],
            )
            sent.append(copy)
            yield
            copy.wait_recv()
            sums[turn, k + 1] = sums[turn, k] + sums_in[turn, k]
        for copy in sent:
            copy.wait_send()

    def scalar(turn, k):
        return jnp.sum(sums[turn, STEPS, k], keepdims=True)

    started = []
    tasks = {}
    zero = jnp.zeros((8, LANES), F32)

    def drain(name):
        for _ in tasks.get(name, ()):
            pass

    def weigh(wave, field):
        curve = zero
        for k in range(2):
            w = w_all[k, wave, 0:1]
            u = w * field[wave, k]
            out[wave, own_place(wave) + k] = u.astype(BF16)
            curve += 0.5 * folded(u * field[wave, k])
        return curve

    sums[0, 0] = jnp.zeros((2, 8, LANES), F32)
    sums[1, 0] = jnp.zeros((2, 8, LANES), F32)
    sums[2, 0] = jnp.zeros((2, 8, LANES), F32)

    def first_norms():
        def step(i, carry):
            square = folded(b_ref[i] * b_ref[i])
            return carry[0] + square, carry[1] + d_ref[i] * square
        rr, bdb = lax.fori_loop(0, 2 * OWN, step, (zero, zero))
        sums[0, 0, 0] = rr
        sums[0, 0, 1] += bdb

    def run(wave):
        yield from sens_forward(wave)
        yield from reduce_field(wave, field0)
        if wave == 0:
            w_copy.wait()
        sums[0, 0, 1] += weigh(wave, field0)
        yield "weighed"
        yield from spread(wave)
        yield from sens_back(wave, image0)

        def step(i, _):
            at_ = 2 * i + wave
            image = image0[at_] + d_ref[at_] * b_ref[at_]
            image0[at_] = image
            spectra[wave, s, i] = image.astype(BF16)
            return 0
        lax.fori_loop(0, OWN, step, 0, unroll=2)
        yield "image"
        yield from sens_forward(wave)
        yield from reduce_field(wave, field1)
        yield "field"
        drain("second")
        alpha, beta = coefficients()
        for k in range(2):
            field1[wave, k] = (1.0 + beta) * field0[wave, k] - alpha * field1[wave, k]
        sums[2, 0, 0] += weigh(wave, field1)
        yield "weighed"
        yield from spread(wave)
        yield from sens_back(wave, image1)

    def coefficients():
        rr0 = scalar(0, 0)
        return rr0 / scalar(0, 1), scalar(1, 0) / rr0

    def second_norm():
        drain("first")
        alpha = scalar(0, 0) / scalar(0, 1)

        def step(i, carry):
            residual = b_ref[i] - alpha * image0[i]
            return carry + folded(residual * residual)
        sums[1, 0, 0] = lax.fori_loop(0, 2 * OWN, step, zero)

    def third_norm():
        alpha, beta = coefficients()

        def step(i, carry):
            p = (1.0 + beta) * b_ref[i] - alpha * image0[i]
            return carry + d_ref[i] * folded(p * p)
        sums[2, 0, 0] += lax.fori_loop(0, 2 * OWN, step, zero)

    waves = [run(0), run(1)]
    seen = []
    alive = [True, True]
    first = True
    while any(alive):
        for wave in range(WAVES):
            if not alive[wave]:
                continue
            try:
                mark = next(waves[wave])
            except StopIteration:
                alive[wave] = False
                continue
            if mark:
                seen.append(mark)
                if mark == "weighed" and seen.count(mark) == 2:
                    tasks["first"] = total_of(0)
                if mark == "image" and seen.count(mark) == 2:
                    second_norm()
                    tasks["second"] = total_of(1)
                if mark == "weighed" and seen.count(mark) == 4:
                    third_norm()
                    tasks["third"] = total_of(2)
        if first:
            first_norms()
            first = False
        for task in tasks.values():
            next(task, None)

    drain("third")
    alpha, beta = coefficients()
    alpha1 = scalar(1, 0) / scalar(2, 0)

    def finish(i, _):
        residual = b_ref[i] - alpha * image0[i]
        p = residual + beta * b_ref[i]
        sol_ref[i] = alpha * b_ref[i] + alpha1 * p
        res_ref[i] = residual - alpha1 * (image1[i] + d_ref[i] * p)
        return 0
    lax.fori_loop(0, 2 * OWN, finish, 0, unroll=2)


def body(operator, right_side, noise_weights, damping):
    shape = right_side.shape
    op = operator.reshape(128, 256, LANES)
    b = right_side.reshape(2 * OWN, ROWS, LANES)
    block = (ROWS, LANES)
    vmem = pl.BlockSpec(memory_space=pltpu.VMEM)
    dma = pltpu.SemaphoreType.DMA
    scratch = [
        pltpu.VMEM((128, 256, LANES), BF16),
        pltpu.VMEM((WAVES, NS, OWN, *block), BF16),
        pltpu.VMEM((WAVES, 64, *block), BF16),
        pltpu.VMEM((WAVES, 16, *block), BF16),
        pltpu.VMEM((WAVES, 2, *block), F32),
        pltpu.VMEM((WAVES, 2, *block), F32),
        pltpu.VMEM((WAVES, 64, *block), BF16),
        pltpu.VMEM((WAVES, NS, OWN, *block), BF16),
        pltpu.VMEM((WAVES, 2, OWN, *block), BF16),
        pltpu.VMEM((WAVES, OWN, *block), BF16),
        pltpu.VMEM((WAVES, 2, *block), BF16),
        pltpu.VMEM((WAVES, 2, *block), BF16),
        pltpu.VMEM((2 * OWN, *block), F32),
        pltpu.VMEM((2 * OWN, *block), F32),
        pltpu.VMEM((2, 2, 8, LANES), F32),
        pltpu.VMEM((2, 2, 16, *block), BF16),
        pltpu.VMEM((2, 4, 2, *block), BF16),
        pltpu.VMEM((2, 4, 8, *block), BF16),
        pltpu.VMEM((2, 2, 2, *block), BF16),
        pltpu.VMEM((3, STEPS + 1, 2, 8, LANES), F32),
        pltpu.VMEM((3, STEPS, 2, 8, LANES), F32),
        dma, dma((WAVES, 6)), dma((WAVES, 6)),
        dma((WAVES, 2, 2, 4, 2)), dma((WAVES, 2, 2, 4, 2)),
        dma((WAVES, 2, 2, 4, 2)), dma((WAVES, 2, 2, 4, 2)),
        dma((WAVES,)), dma((WAVES,)), dma, dma, dma((3, STEPS)), dma((3, STEPS)),
    ]
    result = jax.ShapeDtypeStruct(b.shape, F32)
    sol, res = pl.pallas_call(
        kernel,
        out_shape=(result, result),
        in_specs=[
            pl.BlockSpec(memory_space=pl.ANY), vmem, vmem,
            pl.BlockSpec(memory_space=pltpu.SMEM),
        ],
        out_specs=(vmem, vmem),
        scratch_shapes=scratch,
        compiler_params=pltpu.CompilerParams(
            collective_id=0, has_side_effects=True, vmem_limit_bytes=56 * 2**20
        ),
        name="solve",
    )(op, b, noise_weights, damping)
    return sol.reshape(shape), res.reshape(shape)


def solution(mesh):
    sides = P("sens", None, None, "src")
    return jax.shard_map(
        body,
        mesh=mesh,
        in_specs=(P(None, None, "sens", "src"), sides, P("src", "sens"), P("sens")),
        out_specs=(sides, sides),
        check_vma=False,
    )
```

time: 623 us -> 203 us (0.33)
  blocking collectives: 230 us -> 0 us
  waiting for transfers between devices: 219 us -> 0 us
  Pallas kernels: 0 us -> 197 us
  local copies, waits for them, and re-layouts: 99.8 us -> 4.61 us
  starting transfers between devices: 29.3 us -> 0 us
  matrix products: 20.2 us -> 0 us
  other arithmetic: 16.4 us -> 0 us
    all_to_all x5 -> x0, waiting for transfers between devices: 219 us -> none  [the longest x2 181 us: exchange_in_pieces(): lax.all_to_all(share, axis, split_axis=0, concat_axis=0, tiled=True)]
    pallas_call x0 -> x1, Pallas kernels: none -> 197 us  [body(): pl.pallas_call(kernel, out_shape=(result, result), in_specs=[pl.BlockSpec...]
    all_to_all x6 -> x0, blocking collectives: 147 us -> none  [the longest x2 47.5 us: in_one_piece(): lax.all_to_all(both, axis, split_axis=split_dim, concat_axis=concat_dim,...]
    psum x10 -> x0, blocking collectives: 83.6 us -> none  [by_axis(): return functools.reduce(lax.psum, axes, value)]
    unnamed x23 -> x2, local copies, waits for them, and re-layouts: 43.1 us -> 4.61 us
    all_to_all x5 -> x0, starting transfers between devices: 29.3 us -> none  [the longest x2 15 us: exchange_in_pieces(): lax.all_to_all(share, axis, split_axis=0, concat_axis=0, tiled=True)]
    dot_general x16 -> x0, matrix products: 20.2 us -> none  [the longest x2 5.38 us: forward_all(): jnp.einsum('fms,frs->frm', gmat[:, 0], vector[:, 0], preferred_element_ty...]
    all_to_all x7 -> x0, local copies, waits for them, and re-layouts: 20.1 us -> none  [the longest x2 18.4 us: in_one_piece(): lax.all_to_all(both, axis, split_axis=split_dim, concat_axis=concat_dim,...]
  transfers between devices with their start and end apart: 5 -> 0, of which waited for: 4 -> 0; matrix products, arithmetic and copies ran while one was open for 6% -> 0% of each run, Pallas kernels for 0% -> 0%
where the time goes in v1:
time: 203 us; the launch traced here: 202 us
  Pallas kernels  197 us (97%)
  local copies, waits for them, and re-layouts  4.61 us (2%)
    pallas_call x1, Pallas kernels, body(): pl.pallas_call(kernel, out_shape=(result, result), in_specs=[pl.BlockSpec...  197 us
    unnamed x2, local copies, waits for them, and re-layouts  4.61 us

profile of v1, /device:TPU:2, one launch (start us, length us, event | category | flops | bytes accessed | tf_op | source)
XLA Modules:
  0.0 201.9 jit_solution(14701989429513037989)
XLA Ops:
  0.6 196.7 %solve.1 = (f32[32,64,128]{2,1,0:T(8,128)}, f32[32,64,128]{2,1,0:T(8,128)}) custom-call(bf16[128,256,128]{2,1,0:T(8,128)(2,1)} %bitcast.4, f32[32,64,128]{2,1,0:T(8,128)} %bitcast.5, f32[2,128]{1,0:T(2,128)} %w_ref.1, f32[32]{0:T(128)} %d_ref.1), custom_call_target="tpu_custom_call" | custom-call | tf_op jit(solution)/shard_map/solve/pallas_call | solution.py:482
  197.3 2.3 %copy.8 = f32[32,2,32,128]{3,2,1,0:T(8,128)} copy(f32[32,2,32,128]{3,2,1,0:T(8,128)} %bitcast.7) | data formatting | bytes 2097152
  199.6 2.3 %copy.9 = f32[32,2,32,128]{3,2,1,0:T(8,128)} copy(f32[32,2,32,128]{3,2,1,0:T(8,128)} %bitcast.6) | data formatting | bytes 2097152

commit v2 on v1

v2 whole, which is shorter than its diff:
```python
import functools

import jax
import jax.numpy as jnp
from jax import lax
from jax.experimental import pallas as pl
from jax.experimental.pallas import tpu as pltpu
from jax.sharding import PartitionSpec as P

BF16, F32 = jnp.bfloat16, jnp.float32
MESH = pl.DeviceIdType.MESH
NZ, NX, NY, NS = 8, 2, 4, 4
LIMIT = 51
SPLIT = 2
WAVES, ROWS, LANES = 2 * SPLIT, 64 // SPLIT, 128
HALF = ROWS // 2
OWN = 16
AXES = (("y", "z"), ("z", "y")) * SPLIT
SIZE = {"y": NY, "z": NZ}
MESSAGES, LAST = 13, 5


def flip(value, bit):
    return value + bit - 2 * bit * lax.rem(lax.div(value, bit), 2)


RATE = {"x": 46.0e3, "y": 46.0e3, "z": 46.0e3, "core": 250.0e3, "xh": 46.0e3}
DELAY = {"x": 1.7, "y": 1.7, "z": 1.7, "core": 0.9, "xh": 2.5}
BLOCK = ROWS * LANES * 2


class Plan:
    def __init__(self):
        self.now, self.free, self.done = 0.0, {}, {}

    def spend(self, time):
        self.now += time

    def sent(self, link, way, size):
        begin = max(self.now, self.free.get((link, way), 0.0))
        self.free[link, way] = begin + size / RATE.get(link, 46.0e3)
        return self.free[link, way] + DELAY[link]

    def due(self, mark):
        return self.done.get(mark, float("inf")) if isinstance(mark, str) else mark

    def run(self, tasks):
        waiting = [[task, 0.0] for task in tasks]
        while waiting:
            entry = min(waiting, key=lambda pair: self.due(pair[1]))
            self.now = max(self.now, self.due(entry[1]))
            assert self.now < float("inf")
            value = next(entry[0], None)
            if value is None:
                waiting.remove(entry)
            elif isinstance(value, (str, float)):
                entry[1] = value
            else:
                waiting.append([value, 0.0])


def kernel(
    op_hbm, b_hbm, w_ref, d_ref, image0, image1, scalars,
    op, b_ref, spectra, part, part2, field0, field1, out, grad, core_in, x_in, xh_out, xh_in,
    w_all, ring_ya, ring_zb, ring_za, ring_yb, sums, sums_in,
    op_sem, b_sem, sens_s, sens_r, rs_s, rs_r, ag_s, ag_r, xh_s, xh_r, w_s, w_r, sum_s, sum_r,
):
    plan = Plan()
    s, q = lax.axis_index("sens"), lax.axis_index("src")
    z, xh, y = lax.div(q, 8), lax.rem(lax.div(q, 4), 2), lax.rem(q, 4)
    at = {"y": y, "z": z}
    rings = ((ring_ya, ring_zb), (ring_za, ring_yb))

    def device(s=s, z=z, xh=xh, y=y):
        return (s, z * 8 + xh * 4 + y)

    def along(axis, step):
        n = SIZE[axis]
        return device(**{axis: lax.rem(at[axis] + n + step, n)})

    core_peer, x_peer, xh_peer = device(s=flip(s, 1)), device(s=flip(s, 2)), device(xh=1 - xh)
    greeted = (
        core_peer, x_peer, xh_peer, along("y", 1), along("y", -1), along("z", 1), along("z", -1),
    )

    def copy_of(src, dst, send_sem, recv_sem, to):
        return pltpu.make_async_remote_copy(
            src_ref=src, dst_ref=dst, send_sem=send_sem, recv_sem=recv_sem,
            device_id=to, device_id_type=MESH,
        )

    unsettled = {}

    def begin(name, copy, link, way, size):
        copy.start()
        unsettled.setdefault(name, []).append(copy)
        return plan.sent(link, way, size)

    def settle(name):
        for copy in unsettled.pop(name, ()):
            copy.wait_send()

    b_load = pltpu.make_async_copy(b_hbm, b_ref, b_sem)
    b_load.start()
    load = pltpu.make_async_copy(op_hbm, op, op_sem)
    load.start()
    barrier = pltpu.get_barrier_semaphore()
    for peer in greeted:
        pl.semaphore_signal(barrier, inc=1, device_id=peer, device_id_type=MESH)

    def rows(ref, i, wave):
        low = HALF * (wave // 2)
        parts = [ref[i, pl.ds(low, HALF)], ref[i, pl.ds(32 + low, HALF)]]
        return jnp.concatenate(parts, axis=0)

    def round_own(wave):
        def step(i, _):
            spectra[wave, s, i] = rows(b_ref, 2 * i + wave % 2, wave).astype(BF16)
            return 0
        lax.fori_loop(0, OWN, step, 0)

    b_load.wait()
    for wave in range(WAVES):
        round_own(wave)
    w_all[xh] = jnp.broadcast_to(w_ref[...][:, None, :], (2, 8, LANES))
    pl.semaphore_wait(barrier, len(greeted))

    def place(wave, zz, xx, yy):
        return yy * 16 + zz * 2 + xx if wave % 2 == 0 else zz * 8 + yy * 2 + xx

    def indices(block, i):
        return 2 * block + lax.div(i, 8), lax.rem(lax.div(i, 4), 2), lax.rem(i, 4)

    def forward(wave, one, two):
        def step(j, _):
            block, i = one + (two - one) * lax.div(j, OWN), lax.rem(j, OWN)
            zz, xx, yy = indices(block, i)
            out_ = lax.dot_general(
                spectra[wave, block, i], op[16 * zz + 8 * xx + 2 * yy + wave % 2],
                (((1,), (1,)), ((), ())), preferred_element_type=F32,
            )
            real = out_[:HALF, :LANES] - out_[HALF:, LANES:]
            imag = out_[HALF:, :LANES] + out_[:HALF, LANES:]
            part[wave, place(wave, zz, xx, yy)] = jnp.concatenate([real, imag], axis=0).astype(BF16)
            return 0
        lax.fori_loop(0, 2 * OWN, step, 0, unroll=16)
        plan.spend(1.4 / SPLIT + 0.2)

    def adjoint(wave, one, two):
        def step(j, _):
            block, i = one + (two - one) * lax.div(j, OWN), lax.rem(j, OWN)
            zz, xx, yy = indices(block, i)
            u = out[wave, place(wave, zz, xx, yy)]
            turned = jnp.concatenate([u[HALF:], -u[:HALF]], axis=0)
            f = 16 * zz + 8 * xx + 2 * yy + wave % 2
            g = jnp.dot(u, op[f, :LANES], preferred_element_type=F32)
            g += jnp.dot(turned, op[f, LANES:], preferred_element_type=F32)
            grad[wave, block, i] = g.astype(BF16)
            return 0
        lax.fori_loop(0, 2 * OWN, step, 0, unroll=16)
        plan.spend(1.4 / SPLIT + 0.2)

    def sens_begin(wave):
        mine, far = s, flip(s, 2)

        def move(k, block, to):
            ref = spectra.at[wave, block]
            return copy_of(ref, ref, sens_s.at[wave, k], sens_r.at[wave, k], to)

        size, name = OWN * BLOCK, ("spectra", wave)
        eta_x = begin(name, move(0, mine, x_peer), "x", 1, size)
        eta_core = begin(name, move(1, mine, core_peer), "core", 1, size)
        return eta_x, eta_core, move

    def sens_forward(wave, begun):
        mine, core, far, both = s, flip(s, 1), flip(s, 2), flip(flip(s, 1), 2)
        eta_x, eta_core, move = begun
        settle(("part", wave))
        settle(("out", wave))
        if not loaded:
            load.wait()
            loaded.append(True)
        yield eta_core
        move(1, core, core_peer).wait_recv()
        forward(wave, mine, core)
        yield eta_x
        move(0, far, x_peer).wait_recv()
        yield begin(("spectra", wave), move(2, far, core_peer), "core", 1, OWN * BLOCK)
        move(2, both, core_peer).wait_recv()
        forward(wave, far, both)

    def ring_sum(wave, level, ref, result, name):
        axis = AXES[wave][level]
        n, me = SIZE[axis], at[axis]
        piece = ref.shape[0] // n
        half, ring = piece // 2, rings[wave % 2][level].at[wave // 2]
        eta = {}

        top = n // 2

        def span(h):
            return (0, piece) if h is None else (h * half, half)

        def message(t, h, k):
            d = (1, -1)[k]
            dest = lax.rem(me + n + d * t, n)
            low, size = span(h)
            sems = (wave, level, k, t - 1, h or 0)
            return copy_of(
                ref.at[pl.ds(dest * piece + low, size)], ring.at[k, t - 1, pl.ds(low, size)],
                rs_s.at[sems], rs_r.at[sems], along(axis, d),
            )

        def go(t, h, k):
            eta[t, h, k] = begin(name, message(t, h, k), axis, k, span(h)[1] * BLOCK)

        def add(t, h, k):
            message(t, h, k).wait_recv()
            dest = lax.rem(me + n + (1, -1)[k] * (t - 1), n)
            low, size = span(h)

            def step(i, _):
                at_ = dest * piece + low + i
                total = ref[at_].astype(F32) + ring[k, t - 1, low + i].astype(F32)
                ref[at_] = total.astype(BF16)
                return 0
            lax.fori_loop(0, size, step, 0, unroll=min(size, 2))
            plan.spend(0.1 + 0.01 * size / SPLIT)

        for k in (0, 1):
            go(top, k, k)
        if level == 0:
            for k in (0, 1):
                go(top - 1, 1 - k, k)
        for t in range(top, 1, -1):
            whole = level == 1
            for k in (0, 1):
                h = k if t == top or not whole else None
                yield eta[t, h, k]
                add(t, h, k)
                go(t - 1, None if whole else k, k)
            if t - 1 > 1 and not whole:
                for k in (0, 1):
                    yield eta[t - 1, 1 - k, k]
                    add(t - 1, 1 - k, k)
                    go(t - 2, 1 - k, k)
        final = [(1, h, k) for h in ((None,) if level == 1 else (0, 1)) for k in (0, 1)]
        yield max(eta[key] for key in final)
        for key in final:
            message(*key).wait_recv()

        def last(i, _):
            total = ref[me * piece + i].astype(F32) + ring[0, 0, i].astype(F32)
            result(i, total + ring[1, 0, i].astype(F32))
            return 0
        lax.fori_loop(0, piece, last, 0, unroll=2)
        plan.spend(0.1 + 0.015 * piece / SPLIT)

    def ring_gather(wave, level, ref):
        axis = AXES[wave][level]
        n, me = SIZE[axis], at[axis]
        piece = ref.shape[0] // n
        half = piece // 2
        eta = {}
        top = n // 2

        def message(t, h, k, owner):
            low, size = (0, piece) if h is None else (h * half, half)
            sems = (wave, level, k, t - 1, h or 0)
            where = ref.at[pl.ds(owner * piece + low, size)]
            return copy_of(where, where, ag_s.at[sems], ag_r.at[sems], along(axis, (1, -1)[k]))

        def go(t, h, k):
            copy = message(t, h, k, lax.rem(me + n - (1, -1)[k] * (t - 1), n))
            size = (piece if h is None else half) * BLOCK
            eta[t, h, k] = begin(("out", wave), copy, axis, k, size)

        def got(t, h, k):
            message(t, h, k, lax.rem(me + n - (1, -1)[k] * t, n)).wait_recv()

        if level == 1:
            for k in (0, 1):
                go(1, None, k)
            for t in range(1, top):
                for k in (0, 1):
                    yield eta[t, None, k]
                    got(t, None, k)
                    go(t + 1, None if t + 1 < top else k, k)
        else:
            for first in (0, 1):
                for k in (0, 1):
                    go(1, k if first == 0 else 1 - k, k)
            for t in range(1, top):
                for k in (0, 1):
                    yield eta[t, k, k]
                    got(t, k, k)
                    go(t + 1, k, k)
                for k in (0, 1):
                    if t + 1 < top:
                        yield eta[t, 1 - k, k]
                        got(t, 1 - k, k)
                        go(t + 1, 1 - k, k)
        yield max(eta[top, k, k] for k in (0, 1))
        if level == 0:
            for k in (0, 1):
                got(top - 1, 1 - k, k)
        for k in (0, 1):
            got(top, k, k)

    def reduce_field(wave, field):
        def keep2(i, total):
            part2[wave, i] = total.astype(BF16)

        def keep1(i, total):
            xh_out[wave, i] = total.astype(BF16)

        settle(("part2", wave))
        settle(("xh", wave))
        yield from ring_sum(wave, 0, part.at[wave], keep2, ("part", wave))
        share = part2.at[wave, pl.ds(0, 64 // SIZE[AXES[wave][0]])]
        yield from ring_sum(wave, 1, share, keep1, ("part2", wave))
        copy = copy_of(xh_out.at[wave], xh_in.at[wave], xh_s.at[wave], xh_r.at[wave], xh_peer)
        yield begin(("xh", wave), copy, "xh", 1, 2 * BLOCK)
        copy.wait_recv()
        field[wave] = xh_out[wave].astype(F32) + xh_in[wave].astype(F32)

    def spread(wave):
        outer = AXES[wave][0]
        share = 64 // SIZE[outer]
        own = out.at[wave, pl.ds(at[outer] * share, share)]
        yield from ring_gather(wave, 1, own)
        yield from ring_gather(wave, 0, out.at[wave])

    def sens_back(wave, image):
        mine, core, far, both = s, flip(s, 1), flip(s, 2), flip(flip(s, 1), 2)
        name, size = ("grad", wave), OWN * BLOCK

        def to_core(k, block):
            return copy_of(
                grad.at[wave, block], core_in.at[wave, k],
                sens_s.at[wave, 3 + k], sens_r.at[wave, 3 + k], core_peer,
            )

        settle(name)
        settle(("spectra", wave))
        adjoint(wave, both, far)
        first = to_core(0, both)
        eta = begin(name, first, "core", 1, size)
        yield eta
        first.wait_recv()

        def chip(i, _):
            total = grad[wave, far, i].astype(F32) + core_in[wave, 0, i].astype(F32)
            grad[wave, far, i] = total.astype(BF16)
            return 0
        lax.fori_loop(0, OWN, chip, 0, unroll=2)
        plan.spend(0.1 + 0.2 / SPLIT)
        across = copy_of(
            grad.at[wave, far], x_in.at[wave], sens_s.at[wave, 5], sens_r.at[wave, 5], x_peer
        )
        eta = begin(name, across, "x", 1, size)
        adjoint(wave, core, mine)
        second = to_core(1, core)
        begin(name, second, "core", 1, size)
        yield eta
        second.wait_recv()
        across.wait_recv()

        def whole(i, _):
            total = grad[wave, mine, i].astype(F32) + core_in[wave, 1, i].astype(F32)
            total += x_in[wave, i].astype(F32)
            at_ = 2 * i + wave % 2
            if image is image0:
                total += d_ref[at_] * rows(b_ref, at_, wave)
                spectra[wave, s, i] = total.astype(BF16)
            low = HALF * (wave // 2)
            image[at_, pl.ds(low, HALF)] = total[:HALF]
            image[at_, pl.ds(32 + low, HALF)] = total[HALF:]
            return 0
        lax.fori_loop(0, OWN, whole, 0, unroll=2)
        plan.spend(0.1 + 0.3 / SPLIT)

    def folded(value):
        return jnp.sum(value.reshape(-1, 8, LANES), axis=0)

    def total_of(turn):
        def message(m, source, to):
            return copy_of(
                source, sums_in.at[turn, m], sum_s.at[turn, m], sum_r.at[turn, m], to
            )

        for m, (link, peer) in enumerate((("core", core_peer), ("x", x_peer), ("xh", xh_peer))):
            copy = message(m, sums.at[turn, m], peer)
            yield begin("sums", copy, link, 1, 8192)
            copy.wait_recv()
            sums[turn, m + 1] = sums[turn, m] + sums_in[turn, m]
        m, level = 3, 3
        for axis in ("y", "z"):
            top = SIZE[axis] // 2
            total = sums[turn, level]
            last = [sums.at[turn, level]] * 2
            for t in range(1, top + 1):
                ways = (0, 1) if t < top else (0,)
                copies = []
                for k in ways:
                    copy = message(m, last[k], along(axis, (1, -1)[k]))
                    eta = begin("sums", copy, axis, k, 8192)
                    copies.append(copy)
                    last[k] = sums_in.at[turn, m]
                    m += 1
                yield eta
                for k in ways:
                    copies[k].wait_recv()
                    total = total + last[k][...]
            level += 1
            sums[turn, level] = total
        plan.done["total%d" % turn] = plan.now

    def scalar(turn, k):
        return jnp.sum(sums[turn, LAST, k], keepdims=True)

    loaded = []
    counts = {}
    zero = jnp.zeros((8, LANES), F32)

    def arrived(name):
        counts[name] = counts.get(name, 0) + 1
        if counts[name] == WAVES:
            plan.done[name] = plan.now

    def weigh(wave, field):
        curve = zero
        for k in range(2):
            w = w_all[k, wave % 2, 0:1]
            u = w * field[wave, k]
            out[wave, place(wave, z, 0, y) + k] = u.astype(BF16)
            curve += 0.5 * folded(u * field[wave, k])
        plan.spend(0.1 + 0.2 / SPLIT)
        return curve

    def coefficients():
        rr0 = scalar(0, 0)
        return rr0 / scalar(0, 1), scalar(1, 0) / rr0

    def run(wave):
        yield from sens_forward(wave, begun[wave])
        yield from reduce_field(wave, field0)
        if "w" not in counts:
            w_copy.wait_recv()
            counts["w"] = 1
        sums[0, 0, 1] += weigh(wave, field0)
        arrived("weighed0")
        yield from spread(wave)
        yield from sens_back(wave, image0)
        now = sens_begin(wave)
        arrived("image")
        yield from sens_forward(wave, now)
        yield from reduce_field(wave, field1)
        yield "total1"
        alpha, beta = coefficients()
        for k in range(2):
            field1[wave, k] = (1.0 + beta) * field0[wave, k] - alpha * field1[wave, k]
        sums[2, 0, 0] += weigh(wave, field1)
        arrived("weighed1")
        yield from spread(wave)
        yield from sens_back(wave, image1)

    def norms():
        yield "weighed0"
        yield from total_of(0)
        yield "image"
        alpha = scalar(0, 0) / scalar(0, 1)

        def second(i, carry):
            residual = b_ref[i] - alpha * image0[i]
            return carry + folded(residual * residual)
        sums[1, 0, 0] = lax.fori_loop(0, 2 * OWN, second, zero)
        plan.spend(1.0)
        yield from total_of(1)
        yield "weighed1"
        alpha, beta = coefficients()

        def third(i, carry):
            p = (1.0 + beta) * b_ref[i] - alpha * image0[i]
            return carry + d_ref[i] * folded(p * p)
        sums[2, 0, 0] += lax.fori_loop(0, 2 * OWN, third, zero)
        plan.spend(1.0)
        yield from total_of(2)

    begun = [sens_begin(wave) for wave in range(WAVES)]
    w_copy = copy_of(w_all.at[xh], w_all.at[xh], w_s, w_r, xh_peer)
    begin("w", w_copy, "xh", 1, 8192)
    for turn in range(3):
        sums[turn, 0] = jnp.zeros((2, 8, LANES), F32)

    def first_norms(i, carry):
        square = folded(b_ref[i] * b_ref[i])
        return carry[0] + square, carry[1] + d_ref[i] * square
    rr, bdb = lax.fori_loop(0, 2 * OWN, first_norms, (zero, zero))
    sums[0, 0, 0] = rr
    sums[0, 0, 1] = bdb
    plan.spend(1.0)

    plan.run([*map(run, range(WAVES)), norms()])
    alpha, beta = coefficients()
    alpha1 = scalar(1, 0) / scalar(2, 0)
    for k, value in enumerate((alpha, beta, alpha1)):
        scalars[k] = jnp.broadcast_to(value, (8, LANES))
    for name in list(unsettled):
        settle(name)


def body(operator, right_side, noise_weights, damping):
    shape = right_side.shape
    op = operator.reshape(128, 256, LANES)
    b = right_side.reshape(2 * OWN, 2 * 32, LANES)
    block = (ROWS, LANES)
    vmem = pl.BlockSpec(memory_space=pltpu.VMEM)
    dma = pltpu.SemaphoreType.DMA
    scratch = [
        pltpu.VMEM((128, 256, LANES), BF16),
        pltpu.VMEM((2 * OWN, 2 * 32, LANES), F32),
        pltpu.VMEM((WAVES, NS, OWN, *block), BF16),
        pltpu.VMEM((WAVES, 64, *block), BF16),
        pltpu.VMEM((WAVES, 16, *block), BF16),
        pltpu.VMEM((WAVES, 2, *block), F32),
        pltpu.VMEM((WAVES, 2, *block), F32),
        pltpu.VMEM((WAVES, 64, *block), BF16),
        pltpu.VMEM((WAVES, NS, OWN, *block), BF16),
        pltpu.VMEM((WAVES, 2, OWN, *block), BF16),
        pltpu.VMEM((WAVES, OWN, *block), BF16),
        pltpu.VMEM((WAVES, 2, *block), BF16),
        pltpu.VMEM((WAVES, 2, *block), BF16),
        pltpu.VMEM((2, 2, 8, LANES), F32),
        pltpu.VMEM((SPLIT, 2, 2, 16, *block), BF16),
        pltpu.VMEM((SPLIT, 2, 4, 2, *block), BF16),
        pltpu.VMEM((SPLIT, 2, 4, 8, *block), BF16),
        pltpu.VMEM((SPLIT, 2, 2, 2, *block), BF16),
        pltpu.VMEM((3, LAST + 1, 2, 8, LANES), F32),
        pltpu.VMEM((3, MESSAGES, 2, 8, LANES), F32),
        dma, dma, dma((WAVES, 6)), dma((WAVES, 6)),
        dma((WAVES, 2, 2, 4, 2)), dma((WAVES, 2, 2, 4, 2)),
        dma((WAVES, 2, 2, 4, 2)), dma((WAVES, 2, 2, 4, 2)),
        dma((WAVES,)), dma((WAVES,)), dma, dma, dma((3, MESSAGES)), dma((3, MESSAGES)),
    ]
    result = jax.ShapeDtypeStruct(b.shape, F32)
    image0, image1, scalars = pl.pallas_call(
        kernel,
        out_shape=(result, result, jax.ShapeDtypeStruct((3, 8, LANES), F32)),
        in_specs=[
            pl.BlockSpec(memory_space=pltpu.HBM), pl.BlockSpec(memory_space=pltpu.HBM), vmem,
            pl.BlockSpec(memory_space=pltpu.SMEM),
        ],
        out_specs=(vmem, vmem, vmem),
        scratch_shapes=scratch,
        compiler_params=pltpu.CompilerParams(
            collective_id=0, has_side_effects=True, vmem_limit_bytes=LIMIT * 2**20
        ),
        name="solve",
    )(op, b, noise_weights, damping)
    alpha, beta, alpha1 = (scalars[k : k + 1, 0:1] for k in range(3))
    d = damping[:, None, None]
    residual = b - alpha * image0
    direction = residual + beta * b
    sol = alpha * b + alpha1 * direction
    res = residual - alpha1 * (image1 + d * direction)
    return sol.reshape(shape), res.reshape(shape)


def solution(mesh):
    sides = P("sens", None, None, "src")
    return jax.shard_map(
        body,
        mesh=mesh,
        in_specs=(P(None, None, "sens", "src"), sides, P("src", "sens"), P("sens")),
        out_specs=(sides, sides),
        check_vma=False,
    )
```

time: 203 us -> 165 us (0.81)
  Pallas kernels: 197 us -> 161 us
  local copies, waits for them, and re-layouts: 4.61 us -> 1.33 us
    pallas_call x1, Pallas kernels: 197 us -> 161 us  [body(): pl.pallas_call(kernel, out_shape=(result, result, jax.ShapeDtypeStruct((3...]
    unnamed x2 -> x6, local copies, waits for them, and re-layouts: 4.61 us -> 1.33 us
where the time goes in v2:
time: 165 us
  Pallas kernels  161 us (98%)
  other arithmetic  1.74 us (1%)
    pallas_call x1, Pallas kernels, body(): pl.pallas_call(kernel, out_shape=(result, result, jax.ShapeDtypeStruct((3...  161 us

profile of v2, /device:TPU:2, one launch (start us, length us, event | category | flops | bytes accessed | tf_op | source)
XLA Modules:
  0.0 165.1 jit_solution(4960211032556061313)
XLA Ops:
  0.6 0.0 copy-start
  0.6 0.6 copy-done
  1.3 0.0 copy-start.1
  1.3 0.7 copy-done.1
  2.0 0.0 copy-start.2
  2.0 161.3 %solve.1 = (f32[32,64,128]{2,1,0:T(8,128)S(1)}, f32[32,64,128]{2,1,0:T(8,128)S(1)}, f32[3,8,128]{2,1,0:T(8,128)S(1)}) custom-call(bf16[128,256,128]{2,1,0:T(8,128)(2,1)} %bitcast.12, f32[32,64,128]{2,1,0:T(8,128)} %bitcast.13, f32[2,128]{1,0:T(2,128)S(1)} %copy-done.1, f32[32]{0:T(128)S(1)} %copy-done), custom_call_target="tpu_custom_call" | custom-call | tf_op jit(solution)/shard_map/solve/pallas_call | solution.py:547
  163.3 0.0 copy-done.2
  163.3 1.7 %multiply_subtract_fusion = (f32[32,64,128]{2,1,0:T(8,128)}, f32[32,64,128]{2,1,0:T(8,128)}) fusion(f32[32,64,128]{2,1,0:T(8,128)S(1)} %get-tuple-element.7, f32[32,64,128]{2,1,0:T(8,128)S(1)} %get-tuple-element.6, f32[32]{0:T(128)S(1)} %copy-done, f32[128]{0:T(128)S(1)} %get-tuple-element.11, f32[128]{0:T(128)S(1)} %get-tuple-element.12, ...), kind=kLoop, calls=%fused_computation | loop fusion | flops 2883584 | bytes 5244544 | tf_op jit(solution)/shard_map/sub | solution.py:566
  (1 shorter events, 0.0 us)
Async XLA Ops:
  0.6 0.7 copy-start
  1.3 0.7 copy-start.1
  2.0 161.3 %copy-start.2 = (f32[32,2,32,128]{3,2,1,0:T(8,128)S(1)}, f32[32,2,32,128]{3,2,1,0:T(8,128)}, u32[]{:S(2)}) copy-start(f32[32,2,32,128]{3,2,1,0:T(8,128)} %param.5) | copy-start | bytes 3145732

commit v3 on v2

--- a/solution.py
+++ b/solution.py
@@ -80,7 +80,8 @@
 
     core_peer, x_peer, xh_peer = device(s=flip(s, 1)), device(s=flip(s, 2)), device(xh=1 - xh)
     greeted = (
-        core_peer, x_peer, xh_peer, along("y", 1), along("y", -1), along("z", 1), along("z", -1),
+        core_peer, x_peer, xh_peer, *(along("y", d) for d in range(1, NY)),
+        *(along("z", d) for d in range(1, NZ)),
     )
 
     def copy_of(src, dst, send_sem, recv_sem, to):
@@ -307,6 +308,59 @@
         for k in (0, 1):
             got(top, k, k)
 
+    def direct(wave, ref, sem, name, target, owner):
+        axis = AXES[wave][1]
+        n = SIZE[axis]
+        piece = ref.shape[0] // n
+
+        def message(d, owned):
+            k, t = divmod(d - 1, n // 2)
+            return copy_of(
+                ref.at[pl.ds(owned * piece, piece)], target(k, t, owned * piece, piece),
+                sem[0].at[wave, 1, k, t, 0], sem[1].at[wave, 1, k, t, 0], along(axis, d),
+            )
+
+        etas = []
+        for d in sorted(range(1, n), key=lambda d: -min(d, n - d)):
+            far = min(d, n - d)
+            eta = begin(name, message(d, owner(d)), axis, int(2 * d > n), far * piece * BLOCK)
+            etas.append(eta + 0.75 * (far - 1))
+        return max(etas), message
+
+    def direct_sum(wave, ref, result, name):
+        axis = AXES[wave][1]
+        n, me = SIZE[axis], at[axis]
+        piece = ref.shape[0] // n
+        ring = rings[wave % 2][1].at[wave // 2]
+
+        def dest(d):
+            return lax.rem(me + d, n)
+        eta, message = direct(
+            wave, ref, (rs_s, rs_r), name, lambda k, t, low, size: ring.at[k, t], dest
+        )
+        yield eta
+        for d in range(1, n):
+            message(d, dest(d)).wait_recv()
+        for i in range(piece):
+            total = ref[me * piece + i].astype(F32)
+            for d in range(1, n):
+                k, t = divmod(d - 1, n // 2)
+                total += ring[k, t, i].astype(F32)
+            result(i, total)
+        plan.spend(0.3)
+
+    def direct_gather(wave, ref):
+        axis = AXES[wave][1]
+        n, me = SIZE[axis], at[axis]
+        eta, message = direct(
+            wave, ref, (ag_s, ag_r), ("out", wave),
+            lambda k, t, low, size: ref.at[pl.ds(low, size)], lambda d: me,
+        )
+        yield eta
+        for d in range(1, n):
+            message(d, lax.rem(me + n - d, n)).wait_recv()
+        plan.spend(0.1)
+
     def reduce_field(wave, field):
         def keep2(i, total):
             part2[wave, i] = total.astype(BF16)
@@ -318,7 +372,7 @@
         settle(("xh", wave))
         yield from ring_sum(wave, 0, part.at[wave], keep2, ("part", wave))
         share = part2.at[wave, pl.ds(0, 64 // SIZE[AXES[wave][0]])]
-        yield from ring_sum(wave, 1, share, keep1, ("part2", wave))
+        yield from direct_sum(wave, share, keep1, ("part2", wave))
         copy = copy_of(xh_out.at[wave], xh_in.at[wave], xh_s.at[wave], xh_r.at[wave], xh_peer)
         yield begin(("xh", wave), copy, "xh", 1, 2 * BLOCK)
         copy.wait_recv()
@@ -328,7 +382,7 @@
         outer = AXES[wave][0]
         share = 64 // SIZE[outer]
         own = out.at[wave, pl.ds(at[outer] * share, share)]
-        yield from ring_gather(wave, 1, own)
+        yield from direct_gather(wave, own)
         yield from ring_gather(wave, 0, out.at[wave])
 
     def sens_back(wave, image):
@@ -429,14 +483,21 @@
             plan.done[name] = plan.now
 
     def weigh(wave, field):
-        curve = zero
         for k in range(2):
             w = w_all[k, wave % 2, 0:1]
             u = w * field[wave, k]
             out[wave, place(wave, z, 0, y) + k] = u.astype(BF16)
-            curve += 0.5 * folded(u * field[wave, k])
         plan.spend(0.1 + 0.2 / SPLIT)
-        return curve
+
+    def curve_of(first, second):
+        total = zero
+        for wave in range(WAVES):
+            for k in range(2):
+                y = field0[wave, k]
+                if first is not None:
+                    y = first * y - second * field1[wave, k]
+                total += 0.5 * folded(w_all[k, wave % 2, 0:1] * y * y)
+        return total
 
     def coefficients():
         rr0 = scalar(0, 0)
@@ -448,7 +509,7 @@
         if "w" not in counts:
             w_copy.wait_recv()
             counts["w"] = 1
-        sums[0, 0, 1] += weigh(wave, field0)
+        weigh(wave, field0)
         arrived("weighed0")
         yield from spread(wave)
         yield from sens_back(wave, image0)
@@ -456,17 +517,14 @@
         arrived("image")
         yield from sens_forward(wave, now)
         yield from reduce_field(wave, field1)
-        yield "total1"
-        alpha, beta = coefficients()
-        for k in range(2):
-            field1[wave, k] = (1.0 + beta) * field0[wave, k] - alpha * field1[wave, k]
-        sums[2, 0, 0] += weigh(wave, field1)
+        weigh(wave, field1)
         arrived("weighed1")
         yield from spread(wave)
         yield from sens_back(wave, image1)
 
     def norms():
         yield "weighed0"
+        sums[0, 0, 1] += curve_of(None, None)
         yield from total_of(0)
         yield "image"
         alpha = scalar(0, 0) / scalar(0, 1)
@@ -483,7 +541,7 @@
         def third(i, carry):
             p = (1.0 + beta) * b_ref[i] - alpha * image0[i]
             return carry + d_ref[i] * folded(p * p)
-        sums[2, 0, 0] += lax.fori_loop(0, 2 * OWN, third, zero)
+        sums[2, 0, 0] = curve_of(1.0 + beta, alpha) + lax.fori_loop(0, 2 * OWN, third, zero)
         plan.spend(1.0)
         yield from total_of(2)
 
@@ -563,7 +621,7 @@
     residual = b - alpha * image0
     direction = residual + beta * b
     sol = alpha * b + alpha1 * direction
-    res = residual - alpha1 * (image1 + d * direction)
+    res = residual - alpha1 * ((1.0 + beta) * image0 - alpha * (image1 + d * image0))
     return sol.reshape(shape), res.reshape(shape)
 
 

time: 165 us -> 159 us (0.964)
  Pallas kernels: 161 us -> 155 us
    pallas_call x1, Pallas kernels: 161 us -> 155 us  [body(): pl.pallas_call(kernel, out_shape=(result, result, jax.ShapeDtypeStruct((3...]
where the time goes in v3:
time: 159 us
  Pallas kernels  155 us (97%)
  other arithmetic  1.85 us (1%)
    pallas_call x1, Pallas kernels, body(): pl.pallas_call(kernel, out_shape=(result, result, jax.ShapeDtypeStruct((3...  155 us

profile of v3, /device:TPU:2, one launch (start us, length us, event | category | flops | bytes accessed | tf_op | source)
XLA Modules:
  0.0 159.3 jit_solution(8533184046329736402)
XLA Ops:
  0.6 0.0 copy-start
  0.6 0.6 copy-done
  1.3 0.0 copy-start.1
  1.3 0.7 copy-done.1
  2.0 0.0 copy-start.2
  2.0 155.5 %solve.1 = (f32[32,64,128]{2,1,0:T(8,128)S(1)}, f32[32,64,128]{2,1,0:T(8,128)S(1)}, f32[3,8,128]{2,1,0:T(8,128)S(1)}) custom-call(bf16[128,256,128]{2,1,0:T(8,128)(2,1)} %bitcast.14, f32[32,64,128]{2,1,0:T(8,128)} %bitcast.15, f32[2,128]{1,0:T(2,128)S(1)} %copy-done.1, f32[32]{0:T(128)S(1)} %copy-done), custom_call_target="tpu_custom_call" | custom-call | tf_op jit(solution)/shard_map/solve/pallas_call | solution.py:605
  157.5 0.0 copy-done.2
  157.5 1.8 %multiply_subtract_fusion = (f32[32,64,128]{2,1,0:T(8,128)}, f32[32,64,128]{2,1,0:T(8,128)}) fusion(f32[32,64,128]{2,1,0:T(8,128)S(1)} %get-tuple-element.7, f32[32,64,128]{2,1,0:T(8,128)S(1)} %get-tuple-element.6, f32[32]{0:T(128)S(1)} %copy-done, f32[128]{0:T(128)S(1)} %get-tuple-element.10, f32[128]{0:T(128)S(1)} %get-tuple-element.12, ...), kind=kLoop, calls=%fused_computation | loop fusion | flops 3670016 | bytes 5245056 | tf_op jit(solution)/shard_map/sub | solution.py:624
  (1 shorter events, 0.0 us)
Async XLA Ops:
  0.6 0.7 copy-start
  1.3 0.7 copy-start.1
  2.0 155.5 %copy-start.2 = (f32[32,2,32,128]{3,2,1,0:T(8,128)S(1)}, f32[32,2,32,128]{3,2,1,0:T(8,128)}, u32[]{:S(2)}) copy-start(f32[32,2,32,128]{3,2,1,0:T(8,128)} %param.5) | copy-start | bytes 3145732

commit v4 on v3

--- a/solution.py
+++ b/solution.py
@@ -545,7 +545,7 @@
         plan.spend(1.0)
         yield from total_of(2)
 
-    begun = [sens_begin(wave) for wave in range(WAVES)]
+    begun = {wave: sens_begin(wave) for wave in (1, 0, 3, 2)}
     w_copy = copy_of(w_all.at[xh], w_all.at[xh], w_s, w_r, xh_peer)
     begin("w", w_copy, "xh", 1, 8192)
     for turn in range(3):

time: 159 us -> 158 us (level)
  no operation moved by 1% of the time
where the time goes in v4:
time: 158 us
  Pallas kernels  154 us (97%)
  other arithmetic  1.85 us (1%)
    pallas_call x1, Pallas kernels, body(): pl.pallas_call(kernel, out_shape=(result, result, jax.ShapeDtypeStruct((3...  154 us

profile of v4, /device:TPU:2, one launch (start us, length us, event | category | flops | bytes accessed | tf_op | source)
XLA Modules:
  0.0 158.3 jit_solution(837776998134264268)
XLA Ops:
  0.6 0.0 copy-start
  0.6 0.6 copy-done
  1.3 0.0 copy-start.1
  1.3 0.7 copy-done.1
  2.0 0.0 copy-start.2
  2.0 154.5 %solve.1 = (f32[32,64,128]{2,1,0:T(8,128)S(1)}, f32[32,64,128]{2,1,0:T(8,128)S(1)}, f32[3,8,128]{2,1,0:T(8,128)S(1)}) custom-call(bf16[128,256,128]{2,1,0:T(8,128)(2,1)} %bitcast.14, f32[32,64,128]{2,1,0:T(8,128)} %bitcast.15, f32[2,128]{1,0:T(2,128)S(1)} %copy-done.1, f32[32]{0:T(128)S(1)} %copy-done), custom_call_target="tpu_custom_call" | custom-call | tf_op jit(solution)/shard_map/solve/pallas_call | solution.py:605
  156.4 0.0 copy-done.2
  156.5 1.8 %multiply_subtract_fusion = (f32[32,64,128]{2,1,0:T(8,128)}, f32[32,64,128]{2,1,0:T(8,128)}) fusion(f32[32,64,128]{2,1,0:T(8,128)S(1)} %get-tuple-element.7, f32[32,64,128]{2,1,0:T(8,128)S(1)} %get-tuple-element.6, f32[32]{0:T(128)S(1)} %copy-done, f32[128]{0:T(128)S(1)} %get-tuple-element.10, f32[128]{0:T(128)S(1)} %get-tuple-element.12, ...), kind=kLoop, calls=%fused_computation | loop fusion | flops 3670016 | bytes 5245056 | tf_op jit(solution)/shard_map/sub | solution.py:624
  (1 shorter events, 0.0 us)
Async XLA Ops:
  0.6 0.7 copy-start
  1.3 0.7 copy-start.1
  2.0 154.5 %copy-start.2 = (f32[32,2,32,128]{3,2,1,0:T(8,128)S(1)}, f32[32,2,32,128]{3,2,1,0:T(8,128)}, u32[]{:S(2)}) copy-start(f32[32,2,32,128]{3,2,1,0:T(8,128)} %param.5) | copy-start | bytes 3145732
